TPU v7x, 32 devices: a whole 2x2x4 slice. The times are simulated.
32 devices in a mesh: sec: 8 (over y, x, core), cross: 4 (over z).
Axes of the slice: x: 2, y: 2, z: 4, core: 2. Of those that a mesh axis runs over, the one named last changes fastest.
Arguments:
- rhs_field: float32 [2, 8, 2, 512, 512], P(None, 'sec', None, 'cross'), may hold values from -1.5 to 1.5
- slowness: float32 [8, 512, 512], P('sec', 'cross'), may hold values from 0.25 to 4
- absorb_depth: int32 [8], P('sec'), may hold values from 8 to 64
- line_inverse: bfloat16 [8, 2, 512, 512], P('sec'), may hold values from -1 to 1
- cross_inverse: bfloat16 [8, 2, 512, 512], P('sec', None, 'cross'), may hold values from -1 to 1
Outputs:
- solution: float32 [2, 8, 2, 512, 512], P(None, 'sec', None, 'cross')
- residual: float32 [2, 8, 2, 512, 512], P(None, 'sec', None, 'cross')
All inputs are finite; a program needn't handle non-finite values.
Results may differ from a plain program's by a relative error of at most 0.02.
Values may be sent and summed in bfloat16 or wider, within the bound.
A program may use at most 64 MiB of HBM per device.

v0:
```python
import jax
import jax.numpy as jnp
from jax import lax
from jax.sharding import PartitionSpec as P

SIGMA_TOP = 2.0
CENTER = 128.0 / 30.0
FACE = 14.0 / 30.0
EDGE = 3.0 / 30.0
CORNER = 1.0 / 30.0


def passed_along(shard, axis, by):
    devices = lax.axis_size(axis)
    pairs = [(i, i + by) for i in range(devices) if 0 <= i + by < devices]
    return lax.ppermute(shard, axis, pairs)


def with_halo(cells, sides, width):
    for axis, dim in sides:
        count = lax.axis_size(axis)
        ends = count - 1
        head = lax.slice_in_dim(cells, 0, width, axis=dim)
        tail = lax.slice_in_dim(cells, cells.shape[dim] - width, cells.shape[dim], axis=dim)
        cells = jnp.concatenate(
            [
                lax.ppermute(tail, axis, [(i, (i + 1) % count) for i in range(ends)]),
                cells,
                lax.ppermute(head, axis, [((i + 1) % count, i) for i in range(ends)]),
            ],
            axis=dim,
        )
    return cells


def complex_line(source, matrix):
    real_part = jnp.dot(source[0], matrix[0], preferred_element_type=jnp.float32) - jnp.dot(
        source[1], matrix[1], preferred_element_type=jnp.float32
    )
    imag_part = jnp.dot(source[0], matrix[1], preferred_element_type=jnp.float32) + jnp.dot(
        source[1], matrix[0], preferred_element_type=jnp.float32
    )
    return jnp.stack([real_part, imag_part]).astype(jnp.bfloat16)


def cross_fold(mixed, coupling_rows):
    gathered = lax.all_gather(mixed, "cross", axis=2, tiled=True)
    real_real = jnp.einsum(
        "yk,rkx->ryx", coupling_rows[0], gathered[0], preferred_element_type=jnp.float32
    )
    imag_imag = jnp.einsum(
        "yk,rkx->ryx", coupling_rows[1], gathered[1], preferred_element_type=jnp.float32
    )
    real_imag = jnp.einsum(
        "yk,rkx->ryx", coupling_rows[0], gathered[1], preferred_element_type=jnp.float32
    )
    imag_real = jnp.einsum(
        "yk,rkx->ryx", coupling_rows[1], gathered[0], preferred_element_type=jnp.float32
    )
    real_part = real_real - imag_imag
    imag_part = real_imag + imag_real
    return jnp.stack([real_part, imag_part])


def sweep_section(rhs_local, prior, line_matrix, cross_local):
    item_count = rhs_local.shape[2]
    line_count = rhs_local.shape[3]
    column_count = rhs_local.shape[4]
    source = (rhs_local[:, 0] + prior).astype(jnp.bfloat16)
    mixed = complex_line(source.reshape(2, item_count * line_count, column_count), line_matrix)
    mixed = mixed.reshape(2, item_count, line_count, column_count)
    prior = cross_fold(mixed, cross_local[0])
    outputs = [prior]
    return jnp.stack(outputs, axis=1)


def absorption(absorb_depth, column_count):
    column = jnp.arange(column_count, dtype=jnp.int32)
    distance = jnp.minimum(column, column_count - 1 - column).astype(jnp.float32)
    depth = absorb_depth.astype(jnp.float32)[:, None]
    ramp = jnp.maximum(depth - distance[None, :], 0.0) / depth
    return SIGMA_TOP * ramp * ramp


def operate(field, padded, slowness, absorb_depth):
    layer_count = field.shape[1]
    line_count = field.shape[3]
    column_count = field.shape[4]
    weights = (0.0, FACE, EDGE, CORNER)
    near = jnp.zeros(field.shape, jnp.float32)
    for depth_move in (-1, 0, 1):
        for line_move in (-1, 0, 1):
            for column_move in (-1, 0, 1):
                reach = abs(depth_move) + abs(line_move) + abs(column_move)
                if reach > 0:
                    near = (
                        near
                        + weights[reach]
                        * padded[
                            :,
                            1 + depth_move : 1 + depth_move + layer_count,
                            :,
                            1 + line_move : 1 + line_move + line_count,
                            1 + column_move : 1 + column_move + column_count,
                        ]
                    )
    damping = absorption(absorb_depth, column_count)
    wave_real = slowness[:, None, :, :]
    wave_imag = wave_real * damping[:, None, None, :]
    real_part = CENTER * field[0] - near[0] - (wave_real * field[0] - wave_imag * field[1])
    imag_part = CENTER * field[1] - near[1] - (wave_real * field[1] + wave_imag * field[0])
    return jnp.stack([real_part, imag_part])


def per_device(rhs_field, slowness, absorb_depth, line_inverse, cross_inverse):
    line_matrix = line_inverse[0]
    layer_count = rhs_field.shape[1]
    item_count = rhs_field.shape[2]
    line_count = rhs_field.shape[3]
    column_count = rhs_field.shape[4]
    sections = lax.axis_size("sec")
    start_prior = jnp.zeros((2, item_count, line_count, column_count), jnp.float32)
    first = sweep_section(rhs_field, start_prior, line_matrix, cross_inverse)

    def advance_whole(counter, current):
        prior = passed_along(current[:, layer_count - 1].astype(jnp.bfloat16), "sec", 1).astype(
            jnp.float32
        )
        return sweep_section(rhs_field, prior, line_matrix, cross_inverse)

    solution = lax.fori_loop(0, sections - 1, advance_whole, first)
    padded = with_halo(solution.astype(jnp.bfloat16), (("sec", 1), ("cross", 3)), 1).astype(
        solution.dtype
    )
    padded = jnp.pad(padded, ((0, 0), (0, 0), (0, 0), (0, 0), (1, 1)))
    residual = rhs_field - operate(solution, padded, slowness, absorb_depth)
    return (solution, residual)


def solution(mesh):
    placed = (
        P(None, "sec", None, "cross", None),
        P("sec", "cross", None),
        P("sec"),
        P("sec", None, None, None),
        P("sec", None, "cross", None),
    )
    return jax.shard_map(
        per_device,
        mesh=mesh,
        in_specs=placed,
        out_specs=(P(None, "sec", None, "cross", None), P(None, "sec", None, "cross", None)),
        check_vma=False,
    )
```

profile of v0, /device:TPU:1, one launch (start us, length us, event | category | flops | bytes accessed | tf_op | source)
XLA Modules:
  0.0 556.7 jit_solution(8735741020299506886)
XLA Ops:
  7.2 1.4 convert_element_type.39
  9.8 1.0 fusion.28
  10.8 1.2 copy.21
  13.2 46.5 %all-gather.3.cloned.1.call-done = bf16[2,2,512,512]{2,3,1,0:T(8,128)(2,1)} async-done(((bf16[2,2,128,512]{2,3,1,0:T(8,128)(2,1)}), bf16[2,2,512,512]{2,3,1,0:T(8,128)(2,1)}) %all-gather.3.cloned.1.call-update) | async-done | bytes 2097168 | tf_op jit(solution)/shard_map/all_gather | solution.py:47
  59.7 1.8 fusion.72
  61.6 1.7 fusion.73
  64.2 452.2 %while.10 = (s32[]{:T(128)}, f32[2,1,2,128,512]{3,4,2,0,1:T(8,128)S(1)}, f32[2,1,2,128,512]{3,4,2,0,1:T(8,128)S(1)}, bf16[2,512,512]{2,1,0:T(8,128)(2,1)S(1)}, bf16[1,2,128,512]{3,2,1,0:T(8,128)(2,1)}, /*index=5*/s32[]{:T(128)}) while((s32[]{:T(128)}, f32[2,1,2,128,512]{3,4,2,0,1:T(8,128)S(1)}, f32[2,1,2,128,512]{3,4,2,0,1:T(8,128)S(1)}, ...), condition=%wide.region_1.0_spmd, body=%wide.region_0.0_spmd.sunk | while | flops 1075838976 | bytes 44040396 | solution.py:131
  64.2 1.0 copy.32
  65.2 5.2 collective-permute-start
  70.8 6.1 %collective-permute-done = bf16[2,2,128,512]{3,2,1,0:T(8,128)(2,1)} collective-permute-done((bf16[2,2,128,512]{3,2,1,0:T(8,128)(2,1)}, bf16[2,2,128,512]{3,2,1,0:T(8,128)(2,1)}, u32[]{:S(2)}, u32[]{:S(2)}) %collective-permute-start) | collective-permute-done | bytes 524320 | tf_op jit(solution)/shard_map/while/body/eval_jaxpr/ppermute | solution.py:16
  76.9 1.2 fusion.142
  80.6 43.7 %all-gather.5.cloned.1.call-done = bf16[2,2,512,512]{2,3,1,0:T(8,128)(2,1)} async-done(((bf16[2,2,128,512]{2,3,1,0:T(8,128)(2,1)}), bf16[2,2,512,512]{2,3,1,0:T(8,128)(2,1)}) %all-gather.5.cloned.1.call-update) | async-done | bytes 2097168 | tf_op jit(solution)/shard_map/while/body/eval_jaxpr/all_gather | solution.py:47
  124.3 1.8 fusion.150
  126.2 1.7 fusion.148
  128.8 1.0 copy.32
  129.8 5.2 collective-permute-start
  135.4 6.1 %collective-permute-done = bf16[2,2,128,512]{3,2,1,0:T(8,128)(2,1)} collective-permute-done((bf16[2,2,128,512]{3,2,1,0:T(8,128)(2,1)}, bf16[2,2,128,512]{3,2,1,0:T(8,128)(2,1)}, u32[]{:S(2)}, u32[]{:S(2)}) %collective-permute-start) | collective-permute-done | bytes 524320 | tf_op jit(solution)/shard_map/while/body/eval_jaxpr/ppermute | solution.py:16
  141.5 1.2 fusion.142
  145.2 43.7 %all-gather.5.cloned.1.call-done = bf16[2,2,512,512]{2,3,1,0:T(8,128)(2,1)} async-done(((bf16[2,2,128,512]{2,3,1,0:T(8,128)(2,1)}), bf16[2,2,512,512]{2,3,1,0:T(8,128)(2,1)}) %all-gather.5.cloned.1.call-update) | async-done | bytes 2097168 | tf_op jit(solution)/shard_map/while/body/eval_jaxpr/all_gather | solution.py:47
  188.9 1.8 fusion.150
  190.7 1.7 fusion.148
  193.4 1.0 copy.32
  194.4 5.2 collective-permute-start
  200.0 6.1 %collective-permute-done = bf16[2,2,128,512]{3,2,1,0:T(8,128)(2,1)} collective-permute-done((bf16[2,2,128,512]{3,2,1,0:T(8,128)(2,1)}, bf16[2,2,128,512]{3,2,1,0:T(8,128)(2,1)}, u32[]{:S(2)}, u32[]{:S(2)}) %collective-permute-start) | collective-permute-done | bytes 524320 | tf_op jit(solution)/shard_map/while/body/eval_jaxpr/ppermute | solution.py:16
  206.1 1.2 fusion.142
  209.8 43.7 %all-gather.5.cloned.1.call-done = bf16[2,2,512,512]{2,3,1,0:T(8,128)(2,1)} async-done(((bf16[2,2,128,512]{2,3,1,0:T(8,128)(2,1)}), bf16[2,2,512,512]{2,3,1,0:T(8,128)(2,1)}) %all-gather.5.cloned.1.call-update) | async-done | bytes 2097168 | tf_op jit(solution)/shard_map/while/body/eval_jaxpr/all_gather | solution.py:47
  253.5 1.8 fusion.150
  255.3 1.7 fusion.148
  258.0 1.0 copy.32
  259.0 5.2 collective-permute-start
  264.6 6.1 %collective-permute-done = bf16[2,2,128,512]{3,2,1,0:T(8,128)(2,1)} collective-permute-done((bf16[2,2,128,512]{3,2,1,0:T(8,128)(2,1)}, bf16[2,2,128,512]{3,2,1,0:T(8,128)(2,1)}, u32[]{:S(2)}, u32[]{:S(2)}) %collective-permute-start) | collective-permute-done | bytes 524320 | tf_op jit(solution)/shard_map/while/body/eval_jaxpr/ppermute | solution.py:16
  270.7 1.2 fusion.142
  274.4 43.7 %all-gather.5.cloned.1.call-done = bf16[2,2,512,512]{2,3,1,0:T(8,128)(2,1)} async-done(((bf16[2,2,128,512]{2,3,1,0:T(8,128)(2,1)}), bf16[2,2,512,512]{2,3,1,0:T(8,128)(2,1)}) %all-gather.5.cloned.1.call-update) | async-done | bytes 2097168 | tf_op jit(solution)/shard_map/while/body/eval_jaxpr/all_gather | solution.py:47
  318.1 1.8 fusion.150
  319.9 1.7 fusion.148
  322.6 1.0 copy.32
  323.6 5.2 collective-permute-start
  329.2 6.1 %collective-permute-done = bf16[2,2,128,512]{3,2,1,0:T(8,128)(2,1)} collective-permute-done((bf16[2,2,128,512]{3,2,1,0:T(8,128)(2,1)}, bf16[2,2,128,512]{3,2,1,0:T(8,128)(2,1)}, u32[]{:S(2)}, u32[]{:S(2)}) %collective-permute-start) | collective-permute-done | bytes 524320 | tf_op jit(solution)/shard_map/while/body/eval_jaxpr/ppermute | solution.py:16
  335.3 1.2 fusion.142
  339.0 43.7 %all-gather.5.cloned.1.call-done = bf16[2,2,512,512]{2,3,1,0:T(8,128)(2,1)} async-done(((bf16[2,2,128,512]{2,3,1,0:T(8,128)(2,1)}), bf16[2,2,512,512]{2,3,1,0:T(8,128)(2,1)}) %all-gather.5.cloned.1.call-update) | async-done | bytes 2097168 | tf_op jit(solution)/shard_map/while/body/eval_jaxpr/all_gather | solution.py:47
  382.7 1.8 fusion.150
  384.5 1.7 fusion.148
  387.2 1.0 copy.32
  388.2 5.2 collective-permute-start
  393.8 6.1 %collective-permute-done = bf16[2,2,128,512]{3,2,1,0:T(8,128)(2,1)} collective-permute-done((bf16[2,2,128,512]{3,2,1,0:T(8,128)(2,1)}, bf16[2,2,128,512]{3,2,1,0:T(8,128)(2,1)}, u32[]{:S(2)}, u32[]{:S(2)}) %collective-permute-start) | collective-permute-done | bytes 524320 | tf_op jit(solution)/shard_map/while/body/eval_jaxpr/ppermute | solution.py:16
  399.9 1.2 fusion.142
  403.6 43.7 %all-gather.5.cloned.1.call-done = bf16[2,2,512,512]{2,3,1,0:T(8,128)(2,1)} async-done(((bf16[2,2,128,512]{2,3,1,0:T(8,128)(2,1)}), bf16[2,2,512,512]{2,3,1,0:T(8,128)(2,1)}) %all-gather.5.cloned.1.call-update) | async-done | bytes 2097168 | tf_op jit(solution)/shard_map/while/body/eval_jaxpr/all_gather | solution.py:47
  447.3 1.8 fusion.150
  449.1 1.7 fusion.148
  452.8 5.2 collective-permute-start
  458.4 6.1 %collective-permute-done = bf16[2,2,128,512]{3,2,1,0:T(8,128)(2,1)} collective-permute-done((bf16[2,2,128,512]{3,2,1,0:T(8,128)(2,1)}, bf16[2,2,128,512]{3,2,1,0:T(8,128)(2,1)}, u32[]{:S(2)}, u32[]{:S(2)}) %collective-permute-start) | collective-permute-done | bytes 524320 | tf_op jit(solution)/shard_map/while/body/eval_jaxpr/ppermute | solution.py:16
  464.5 1.2 fusion.142
  468.2 43.7 %all-gather.5.cloned.1.call-done = bf16[2,2,512,512]{2,3,1,0:T(8,128)(2,1)} async-done(((bf16[2,2,128,512]{2,3,1,0:T(8,128)(2,1)}), bf16[2,2,512,512]{2,3,1,0:T(8,128)(2,1)}) %all-gather.5.cloned.1.call-update) | async-done | bytes 2097168 | tf_op jit(solution)/shard_map/while/body/eval_jaxpr/all_gather | solution.py:47
  511.9 1.8 fusion.150
  513.7 1.7 fusion.148
  516.8 5.4 collective-permute-start.1
  522.2 1.9 collective-permute-start.2
  524.8 3.5 collective-permute-done.1
  528.3 7.2 %collective-permute-done.2 = bf16[2,1,2,128,512]{4,3,2,1,0:T(8,128)(2,1)S(1)} collective-permute-done((bf16[2,1,2,128,512]{4,3,2,1,0:T(8,128)(2,1)S(1)}, bf16[2,1,2,128,512]{4,3,2,1,0:T(8,128)(2,1)S(1)}, u32[]{:S(2)}, u32[]{:S(2)}) %collective-permute-start.2) | collective-permute-done | bytes 524320 | tf_op jit(solution)/shard_map/ppermute | solution.py:29
  535.6 1.3 collective-permute-start.3
  536.9 1.3 collective-permute-start.4
  538.2 3.2 collective-permute-done.4
  542.0 5.4 fusion.68
  548.7 1.2 maximum_subtract_fusion
  (161 shorter events, 32.8 us)
Async XLA Ops:
  7.2 1.5 copy-start
  7.2 52.6 %all-gather.3.cloned.1.call-start = ((), (), s32[]{:S(2)}) async-start(), calls=%async_computation | async-start | bytes 2621440 | tf_op jit(solution)/shard_map/all_gather | solution.py:47
  9.6 3.2 copy-start.4
  10.8 48.9 %copy-start.2 = (bf16[1,2,128,512]{3,2,1,0:T(8,128)(2,1)S(1)}, bf16[1,2,128,512]{3,2,1,0:T(8,128)(2,1)}, u32[]{:S(2)}) copy-start(bf16[1,2,128,512]{3,2,1,0:T(8,128)(2,1)} %param.11) | copy-start | bytes 786436
  59.7 3.5 copy-start.7
  64.2 60.2 %all-gather.5.cloned.1.call-start = ((), (), s32[]{:S(2)}) async-start(), calls=%async_computation.1 | async-start | bytes 2621440 | tf_op jit(solution)/shard_map/while/body/eval_jaxpr/all_gather | solution.py:47
  65.2 11.7 %collective-permute-start = (bf16[2,2,128,512]{3,2,1,0:T(8,128)(2,1)}, bf16[2,2,128,512]{3,2,1,0:T(8,128)(2,1)}, u32[]{:S(2)}, u32[]{:S(2)}) collective-permute-start(bf16[2,2,128,512]{3,2,1,0:T(8,128)(2,1)} %bitcast.168), channel_id=1, source_target_pairs={{0,4},{4,8},{8,12},{12,16},{16,20},{20,24},{24,28},{1,5},{5,9},{9,... | collective-permute-start | bytes 1572872 | tf_op jit(solution)/shard_map/while/body/eval_jaxpr/ppermute | solution.py:16
  79.5 44.8 %copy-start.3 = (bf16[1,2,128,512]{3,2,1,0:T(8,128)(2,1)S(1)}, bf16[1,2,128,512]{3,2,1,0:T(8,128)(2,1)}, u32[]{:S(2)}) copy-start(bf16[1,2,128,512]{3,2,1,0:T(8,128)(2,1)} %get-tuple-element.113) | copy-start | bytes 786436 | tf_op jit(solution)/shard_map/while
  124.3 3.5 copy-start.1
  128.8 60.2 %all-gather.5.cloned.1.call-start = ((), (), s32[]{:S(2)}) async-start(), calls=%async_computation.1 | async-start | bytes 2621440 | tf_op jit(solution)/shard_map/while/body/eval_jaxpr/all_gather | solution.py:47
  129.8 11.7 %collective-permute-start = (bf16[2,2,128,512]{3,2,1,0:T(8,128)(2,1)}, bf16[2,2,128,512]{3,2,1,0:T(8,128)(2,1)}, u32[]{:S(2)}, u32[]{:S(2)}) collective-permute-start(bf16[2,2,128,512]{3,2,1,0:T(8,128)(2,1)} %bitcast.168), channel_id=1, source_target_pairs={{0,4},{4,8},{8,12},{12,16},{16,20},{20,24},{24,28},{1,5},{5,9},{9,... | collective-permute-start | bytes 1572872 | tf_op jit(solution)/shard_map/while/body/eval_jaxpr/ppermute | solution.py:16
  144.1 44.8 %copy-start.3 = (bf16[1,2,128,512]{3,2,1,0:T(8,128)(2,1)S(1)}, bf16[1,2,128,512]{3,2,1,0:T(8,128)(2,1)}, u32[]{:S(2)}) copy-start(bf16[1,2,128,512]{3,2,1,0:T(8,128)(2,1)} %get-tuple-element.113) | copy-start | bytes 786436 | tf_op jit(solution)/shard_map/while
  188.9 3.5 copy-start.1
  193.4 60.2 %all-gather.5.cloned.1.call-start = ((), (), s32[]{:S(2)}) async-start(), calls=%async_computation.1 | async-start | bytes 2621440 | tf_op jit(solution)/shard_map/while/body/eval_jaxpr/all_gather | solution.py:47
  194.4 11.7 %collective-permute-start = (bf16[2,2,128,512]{3,2,1,0:T(8,128)(2,1)}, bf16[2,2,128,512]{3,2,1,0:T(8,128)(2,1)}, u32[]{:S(2)}, u32[]{:S(2)}) collective-permute-start(bf16[2,2,128,512]{3,2,1,0:T(8,128)(2,1)} %bitcast.168), channel_id=1, source_target_pairs={{0,4},{4,8},{8,12},{12,16},{16,20},{20,24},{24,28},{1,5},{5,9},{9,... | collective-permute-start | bytes 1572872 | tf_op jit(solution)/shard_map/while/body/eval_jaxpr/ppermute | solution.py:16
  208.7 44.8 %copy-start.3 = (bf16[1,2,128,512]{3,2,1,0:T(8,128)(2,1)S(1)}, bf16[1,2,128,512]{3,2,1,0:T(8,128)(2,1)}, u32[]{:S(2)}) copy-start(bf16[1,2,128,512]{3,2,1,0:T(8,128)(2,1)} %get-tuple-element.113) | copy-start | bytes 786436 | tf_op jit(solution)/shard_map/while
  253.5 3.5 copy-start.1
  258.0 60.2 %all-gather.5.cloned.1.call-start = ((), (), s32[]{:S(2)}) async-start(), calls=%async_computation.1 | async-start | bytes 2621440 | tf_op jit(solution)/shard_map/while/body/eval_jaxpr/all_gather | solution.py:47
  259.0 11.7 %collective-permute-start = (bf16[2,2,128,512]{3,2,1,0:T(8,128)(2,1)}, bf16[2,2,128,512]{3,2,1,0:T(8,128)(2,1)}, u32[]{:S(2)}, u32[]{:S(2)}) collective-permute-start(bf16[2,2,128,512]{3,2,1,0:T(8,128)(2,1)} %bitcast.168), channel_id=1, source_target_pairs={{0,4},{4,8},{8,12},{12,16},{16,20},{20,24},{24,28},{1,5},{5,9},{9,... | collective-permute-start | bytes 1572872 | tf_op jit(solution)/shard_map/while/body/eval_jaxpr/ppermute | solution.py:16
  273.3 44.8 %copy-start.3 = (bf16[1,2,128,512]{3,2,1,0:T(8,128)(2,1)S(1)}, bf16[1,2,128,512]{3,2,1,0:T(8,128)(2,1)}, u32[]{:S(2)}) copy-start(bf16[1,2,128,512]{3,2,1,0:T(8,128)(2,1)} %get-tuple-element.113) | copy-start | bytes 786436 | tf_op jit(solution)/shard_map/while
  318.1 3.5 copy-start.1
  322.6 60.2 %all-gather.5.cloned.1.call-start = ((), (), s32[]{:S(2)}) async-start(), calls=%async_computation.1 | async-start | bytes 2621440 | tf_op jit(solution)/shard_map/while/body/eval_jaxpr/all_gather | solution.py:47
  323.6 11.7 %collective-permute-start = (bf16[2,2,128,512]{3,2,1,0:T(8,128)(2,1)}, bf16[2,2,128,512]{3,2,1,0:T(8,128)(2,1)}, u32[]{:S(2)}, u32[]{:S(2)}) collective-permute-start(bf16[2,2,128,512]{3,2,1,0:T(8,128)(2,1)} %bitcast.168), channel_id=1, source_target_pairs={{0,4},{4,8},{8,12},{12,16},{16,20},{20,24},{24,28},{1,5},{5,9},{9,... | collective-permute-start | bytes 1572872 | tf_op jit(solution)/shard_map/while/body/eval_jaxpr/ppermute | solution.py:16
  337.9 44.8 %copy-start.3 = (bf16[1,2,128,512]{3,2,1,0:T(8,128)(2,1)S(1)}, bf16[1,2,128,512]{3,2,1,0:T(8,128)(2,1)}, u32[]{:S(2)}) copy-start(bf16[1,2,128,512]{3,2,1,0:T(8,128)(2,1)} %get-tuple-element.113) | copy-start | bytes 786436 | tf_op jit(solution)/shard_map/while
  382.7 3.5 copy-start.1
  387.2 60.2 %all-gather.5.cloned.1.call-start = ((), (), s32[]{:S(2)}) async-start(), calls=%async_computation.1 | async-start | bytes 2621440 | tf_op jit(solution)/shard_map/while/body/eval_jaxpr/all_gather | solution.py:47
  388.2 11.7 %collective-permute-start = (bf16[2,2,128,512]{3,2,1,0:T(8,128)(2,1)}, bf16[2,2,128,512]{3,2,1,0:T(8,128)(2,1)}, u32[]{:S(2)}, u32[]{:S(2)}) collective-permute-start(bf16[2,2,128,512]{3,2,1,0:T(8,128)(2,1)} %bitcast.168), channel_id=1, source_target_pairs={{0,4},{4,8},{8,12},{12,16},{16,20},{20,24},{24,28},{1,5},{5,9},{9,... | collective-permute-start | bytes 1572872 | tf_op jit(solution)/shard_map/while/body/eval_jaxpr/ppermute | solution.py:16
  402.5 44.8 %copy-start.3 = (bf16[1,2,128,512]{3,2,1,0:T(8,128)(2,1)S(1)}, bf16[1,2,128,512]{3,2,1,0:T(8,128)(2,1)}, u32[]{:S(2)}) copy-start(bf16[1,2,128,512]{3,2,1,0:T(8,128)(2,1)} %get-tuple-element.113) | copy-start | bytes 786436 | tf_op jit(solution)/shard_map/while
  447.3 3.5 copy-start.1
  451.8 60.2 %all-gather.5.cloned.1.call-start = ((), (), s32[]{:S(2)}) async-start(), calls=%async_computation.1 | async-start | bytes 2621440 | tf_op jit(solution)/shard_map/while/body/eval_jaxpr/all_gather | solution.py:47
  452.8 11.7 %collective-permute-start = (bf16[2,2,128,512]{3,2,1,0:T(8,128)(2,1)}, bf16[2,2,128,512]{3,2,1,0:T(8,128)(2,1)}, u32[]{:S(2)}, u32[]{:S(2)}) collective-permute-start(bf16[2,2,128,512]{3,2,1,0:T(8,128)(2,1)} %bitcast.168), channel_id=1, source_target_pairs={{0,4},{4,8},{8,12},{12,16},{16,20},{20,24},{24,28},{1,5},{5,9},{9,... | collective-permute-start | bytes 1572872 | tf_op jit(solution)/shard_map/while/body/eval_jaxpr/ppermute | solution.py:16
  467.1 44.8 %copy-start.3 = (bf16[1,2,128,512]{3,2,1,0:T(8,128)(2,1)S(1)}, bf16[1,2,128,512]{3,2,1,0:T(8,128)(2,1)}, u32[]{:S(2)}) copy-start(bf16[1,2,128,512]{3,2,1,0:T(8,128)(2,1)} %get-tuple-element.113) | copy-start | bytes 786436 | tf_op jit(solution)/shard_map/while
  511.9 3.5 copy-start.1
  516.7 30.7 %copy-start.6 = (f32[2,1,2,128,512]{4,3,2,1,0:T(8,128)}, f32[2,1,2,128,512]{4,3,2,1,0:T(8,128)S(1)}, u32[]{:S(2)}) copy-start(f32[2,1,2,128,512]{4,3,2,1,0:T(8,128)S(1)} %copy.26) | copy-start | bytes 3145732
  516.7 21.5 %copy-start.8 = (f32[1,128,512]{2,1,0:T(8,128)S(1)}, f32[1,128,512]{2,1,0:T(8,128)}, u32[]{:S(2)}) copy-start(f32[1,128,512]{2,1,0:T(8,128)} %param.8) | copy-start | bytes 786436
  516.8 11.5 %collective-permute-start.1 = (bf16[2,1,2,128,512]{4,3,2,1,0:T(8,128)(2,1)S(1)}, bf16[2,1,2,128,512]{4,3,2,1,0:T(8,128)(2,1)S(1)}, u32[]{:S(2)}, u32[]{:S(2)}) collective-permute-start(bf16[2,1,2,128,512]{4,3,2,1,0:T(8,128)(2,1)S(1)} %convert_element_type.40), channel_id=1, source_target_pairs={{0,4},{4,8},{8,12},{12,16},{16,20},{20,24},{24,28},{1,5},{5,9},{9,... | collective-permute-start | bytes 1572872 | tf_op jit(solution)/shard_map/ppermute | solution.py:27
  522.2 13.3 %collective-permute-start.2 = (bf16[2,1,2,128,512]{4,3,2,1,0:T(8,128)(2,1)S(1)}, bf16[2,1,2,128,512]{4,3,2,1,0:T(8,128)(2,1)S(1)}, u32[]{:S(2)}, u32[]{:S(2)}) collective-permute-start(bf16[2,1,2,128,512]{4,3,2,1,0:T(8,128)(2,1)S(1)} %convert_element_type.40), channel_id=1, source_target_pairs={{4,0},{8,4},{12,8},{16,12},{20,16},{24,20},{28,24},{5,1},{9,5},{13... | collective-permute-start | bytes 1572872 | tf_op jit(solution)/shard_map/ppermute | solution.py:29
  535.6 2.6 collective-permute-start.3
  536.9 4.6 collective-permute-start.4
  547.4 1.2 copy-start.5
Sparse Core Ops, SparseCore 0:
  13.0 46.7 all-gather.2
  80.7 43.5 all-gather.4
  145.3 43.5 all-gather.4
  209.9 43.5 all-gather.4
  274.5 43.5 all-gather.4
  339.1 43.5 all-gather.4
  403.7 43.5 all-gather.4
  468.3 43.5 all-gather.4
where the time goes:
time: 558 us; the launch traced here: 557 us
  waiting for transfers between devices  409 us (73%)
  starting transfers between devices  46.9 us (8%)
  matrix products  44.8 us (8%)
  other arithmetic  24.7 us (4%)
  local copies, waits for them, and re-layouts  15 us (3%)
  between operations  14.9 us (3%)
    all_gather x8, waiting for transfers between devices, cross_fold(): gathered = lax.all_gather(mixed, 'cross', axis=2, tiled=True)  353 us
    ppermute x7, waiting for transfers between devices, passed_along(): return lax.ppermute(shard, axis, pairs)  42.6 us
    ppermute x7, starting transfers between devices, passed_along(): return lax.ppermute(shard, axis, pairs)  36.7 us
    dot_general x8, matrix products, cross_fold(): jnp.einsum('yk,rkx->ryx', coupling_rows[0], gathered[0], preferred_elemen...  14.4 us
    dot_general x8, matrix products, cross_fold(): jnp.einsum('yk,rkx->ryx', coupling_rows[0], gathered[1], preferred_elemen...  13.2 us
  transfers between devices with their start and end apart: 19, of which 18 were waited for; matrix products, arithmetic and copies ran while one was open for 0% of the time, Pallas kernels for 0%

commit v1 on v0

--- a/solution.py
+++ b/solution.py
@@ -8,6 +8,27 @@
 FACE = 14.0 / 30.0
 EDGE = 3.0 / 30.0
 CORNER = 1.0 / 30.0
+
+
+def gather_around(x, axis, dim):
+    size, index, span = (lax.axis_size(axis), lax.axis_index(axis), x.shape[dim])
+    right = [(i, (i + 1) % size) for i in range(size)]
+    behind = [(i, (i - 1) % size) for i in range(size)]
+    whole = jnp.zeros((*x.shape[:dim], size * span, *x.shape[dim + 1 :]), x.dtype)
+    whole = lax.dynamic_update_slice_in_dim(whole, x, index * span, axis=dim)
+    from_left = from_right = x
+    half = size // 2
+    for step in range(1, half + 1):
+        from_left = lax.ppermute(from_left, axis, right)
+        whole = lax.dynamic_update_slice_in_dim(
+            whole, from_left, (index - step) % size * span, axis=dim
+        )
+        if step < size - half:
+            from_right = lax.ppermute(from_right, axis, behind)
+            whole = lax.dynamic_update_slice_in_dim(
+                whole, from_right, (index + step) % size * span, axis=dim
+            )
+    return whole
 
 
 def passed_along(shard, axis, by):
@@ -44,7 +65,7 @@
 
 
 def cross_fold(mixed, coupling_rows):
-    gathered = lax.all_gather(mixed, "cross", axis=2, tiled=True)
+    gathered = gather_around(mixed, "cross", 2)
     real_real = jnp.einsum(
         "yk,rkx->ryx", coupling_rows[0], gathered[0], preferred_element_type=jnp.float32
     )

time: 558 us -> 476 us (0.85)
  waiting for transfers between devices: 409 us -> 207 us
  starting transfers between devices: 46.9 us -> 141 us
  local copies, waits for them, and re-layouts: 15 us -> 66.2 us
  matrix products: 44.8 us -> 28.2 us
  between operations: 14.9 us -> 1.55 us
    all_gather x8 -> x0, waiting for transfers between devices: 353 us -> none  [cross_fold(): gathered = lax.all_gather(mixed, 'cross', axis=2, tiled=True)]
    ppermute x0 -> x24, waiting for transfers between devices: none -> 156 us  [the longest x16 122 us: gather_around(): from_left = lax.ppermute(from_left, axis, right)]
    ppermute x7, starting transfers between devices: 36.7 us -> 90 us  [passed_along(): return lax.ppermute(shard, axis, pairs)]
    ppermute x0 -> x24, starting transfers between devices: none -> 30.7 us  [the longest x8 24.9 us: gather_around(): from_right = lax.ppermute(from_right, axis, behind)]
    dynamic_update_slice x0 -> x24, local copies, waits for them, and re-layouts: none -> 30.4 us  [the longest x16 20.4 us: gather_around(): lax.dynamic_update_slice_in_dim(whole, from_left, (index - step) % size *...]
    while x28 -> x56, local copies, waits for them, and re-layouts: 0.07 us -> 13.5 us
    ppermute x2, starting transfers between devices: 6.67 us -> 17.4 us  [with_halo(): lax.ppermute(tail, axis, [(i, (i + 1) % count) for i in range(ends)])]
    dot_general x8, matrix products: 14.4 us -> 4.66 us  [cross_fold(): jnp.einsum('yk,rkx->ryx', coupling_rows[0], gathered[0], preferred_elemen...]
  transfers between devices with their start and end apart: 19 -> 35, of which waited for: 18 -> 33; matrix products, arithmetic and copies ran while one was open for 0% -> 5% of each run, Pallas kernels for 0% -> 0%
where the time goes in v1:
time: 476 us; the launch traced here: 471 us
  waiting for transfers between devices  207 us (43%)
  starting transfers between devices  141 us (30%)
  local copies, waits for them, and re-layouts  66.2 us (14%)
  matrix products  28.2 us (6%)
  other arithmetic  25.6 us (5%)
    ppermute x16, waiting for transfers between devices, gather_around(): from_left = lax.ppermute(from_left, axis, right)  122 us
    ppermute x7, starting transfers between devices, passed_along(): return lax.ppermute(shard, axis, pairs)  90 us
    ppermute x7, waiting for transfers between devices, passed_along(): return lax.ppermute(shard, axis, pairs)  42.4 us
    ppermute x8, waiting for transfers between devices, gather_around(): from_right = lax.ppermute(from_right, axis, behind)  33.8 us
    ppermute x8, starting transfers between devices, gather_around(): from_right = lax.ppermute(from_right, axis, behind)  24.9 us
    dynamic_update_slice x16, local copies, waits for them, and re-layouts, gather_around(): lax.dynamic_update_slice_in_dim(whole, from_left, (index - step) % size *...  20.4 us
    ppermute x2, starting transfers between devices, with_halo(): lax.ppermute(tail, axis, [(i, (i + 1) % count) for i in range(ends)])  17.4 us
    while x56, local copies, waits for them, and re-layouts  13.5 us
  transfers between devices with their start and end apart: 35, of which 33 were waited for; matrix products, arithmetic and copies ran while one was open for 5% of the time, Pallas kernels for 0%

profile of v1, /device:TPU:1, one launch (start us, length us, event | category | flops | bytes accessed | tf_op | source)
XLA Modules:
  0.0 470.8 jit_solution(690667223698637292)
XLA Ops:
  0.6 1.4 convert_element_type.51
  3.8 1.5 broadcast.92
  6.4 2.1 collective-permute-start.4
  8.5 2.0 collective-permute-start.5
  10.5 12.0 %collective-permute-done.4 = bf16[2,2,128,512]{2,3,1,0:T(8,128)(2,1)} collective-permute-done((bf16[2,2,128,512]{2,3,1,0:T(8,128)(2,1)}, bf16[2,2,128,512]{2,3,1,0:T(8,128)(2,1)}, u32[]{:S(2)}, u32[]{:S(2)}) %collective-permute-start.4) | collective-permute-done | bytes 524320 | tf_op jit(solution)/shard_map/ppermute | solution.py:22
  22.9 1.9 constant_dynamic-update-slice_fusion.6
  24.8 8.5 %collective-permute-done.5 = bf16[2,2,128,512]{2,3,1,0:T(8,128)(2,1)} collective-permute-done((bf16[2,2,128,512]{2,3,1,0:T(8,128)(2,1)}, bf16[2,2,128,512]{2,3,1,0:T(8,128)(2,1)}, u32[]{:S(2)}, u32[]{:S(2)}) %collective-permute-start.5) | collective-permute-done | bytes 524320 | tf_op jit(solution)/shard_map/ppermute | solution.py:27
  33.3 1.9 constant_dynamic-update-slice_fusion.5
  35.2 7.8 %collective-permute-done.6 = bf16[2,2,128,512]{2,3,1,0:T(8,128)(2,1)} collective-permute-done((bf16[2,2,128,512]{2,3,1,0:T(8,128)(2,1)}, bf16[2,2,128,512]{2,3,1,0:T(8,128)(2,1)}, u32[]{:S(2)}, u32[]{:S(2)}) %collective-permute-start.6) | collective-permute-done | bytes 524320 | tf_op jit(solution)/shard_map/ppermute | solution.py:22
  42.9 1.9 constant_dynamic-update-slice_fusion.4
  44.9 1.7 fusion.72
  46.5 1.7 fusion.73
  48.2 1.7 fusion.26
  49.8 1.7 fusion.25
  51.6 380.1 %while.12 = (s32[]{:T(128)}, f32[2,1,2,128,512]{3,4,2,0,1:T(8,128)S(1)}, f32[2,1,2,128,512]{3,4,2,0,1:T(8,128)S(1)}, bf16[2,512,512]{2,1,0:T(8,128)(2,1)S(1)}, b...) while((s32[]{:T(128)}, ...), condition=%wide.region_1.2_spmd, body=%wide.region_0.1_spmd.sunk | while | flops 1076625408 | bytes 49284048 | solution.py:152
  52.7 6.3 %collective-permute-start = (bf16[2,2,128,512]{3,2,1,0:T(8,128)(2,1)}, bf16[2,2,128,512]{3,2,1,0:T(8,128)(2,1)}, u32[]{:S(2)}, u32[]{:S(2)}) collective-permute-start(bf16[2,2,128,512]{3,2,1,0:T(8,128)(2,1)} %bitcast.168), channel_id=1, source_target_pairs={{0,4},{4,8},{8,12},{12,16},{16,20},{20,24},{24,28},{1,5},{5,9},{9,... | collective-permute-start | bytes 1572872 | tf_op jit(solution)/shard_map/while/body/eval_jaxpr/ppermute | solution.py:37
  59.4 6.1 %collective-permute-done = bf16[2,2,128,512]{3,2,1,0:T(8,128)(2,1)} collective-permute-done((bf16[2,2,128,512]{3,2,1,0:T(8,128)(2,1)}, bf16[2,2,128,512]{3,2,1,0:T(8,128)(2,1)}, u32[]{:S(2)}, u32[]{:S(2)}) %collective-permute-start) | collective-permute-done | bytes 524320 | tf_op jit(solution)/shard_map/while/body/eval_jaxpr/ppermute | solution.py:37
  70.8 3.3 collective-permute-start.2
  74.1 12.8 %collective-permute-done.1 = bf16[2,2,128,512]{2,3,1,0:T(8,128)(2,1)} collective-permute-done((bf16[2,2,128,512]{2,3,1,0:T(8,128)(2,1)}, bf16[2,2,128,512]{2,3,1,0:T(8,128)(2,1)}, u32[]{:S(2)}, u32[]{:S(2)}) %collective-permute-start.1) | collective-permute-done | bytes 524320 | tf_op jit(solution)/shard_map/while/body/eval_jaxpr/ppermute | solution.py:22
  86.8 3.7 collective-permute-start.3
  91.8 2.6 collective-permute-done.2
  95.6 7.7 %collective-permute-done.3 = bf16[2,2,128,512]{2,3,1,0:T(8,128)(2,1)} collective-permute-done((bf16[2,2,128,512]{2,3,1,0:T(8,128)(2,1)}, bf16[2,2,128,512]{2,3,1,0:T(8,128)(2,1)}, u32[]{:S(2)}, u32[]{:S(2)}) %collective-permute-start.3) | collective-permute-done | bytes 524320 | tf_op jit(solution)/shard_map/while/body/eval_jaxpr/ppermute | solution.py:22
  108.5 9.5 %collective-permute-start = (bf16[2,2,128,512]{3,2,1,0:T(8,128)(2,1)}, bf16[2,2,128,512]{3,2,1,0:T(8,128)(2,1)}, u32[]{:S(2)}, u32[]{:S(2)}) collective-permute-start(bf16[2,2,128,512]{3,2,1,0:T(8,128)(2,1)} %bitcast.168), channel_id=1, source_target_pairs={{0,4},{4,8},{8,12},{12,16},{16,20},{20,24},{24,28},{1,5},{5,9},{9,... | collective-permute-start | bytes 1572872 | tf_op jit(solution)/shard_map/while/body/eval_jaxpr/ppermute | solution.py:37
  118.4 6.1 %collective-permute-done = bf16[2,2,128,512]{3,2,1,0:T(8,128)(2,1)} collective-permute-done((bf16[2,2,128,512]{3,2,1,0:T(8,128)(2,1)}, bf16[2,2,128,512]{3,2,1,0:T(8,128)(2,1)}, u32[]{:S(2)}, u32[]{:S(2)}) %collective-permute-start) | collective-permute-done | bytes 524320 | tf_op jit(solution)/shard_map/while/body/eval_jaxpr/ppermute | solution.py:37
  129.8 3.3 collective-permute-start.2
  133.1 12.8 %collective-permute-done.1 = bf16[2,2,128,512]{2,3,1,0:T(8,128)(2,1)} collective-permute-done((bf16[2,2,128,512]{2,3,1,0:T(8,128)(2,1)}, bf16[2,2,128,512]{2,3,1,0:T(8,128)(2,1)}, u32[]{:S(2)}, u32[]{:S(2)}) %collective-permute-start.1) | collective-permute-done | bytes 524320 | tf_op jit(solution)/shard_map/while/body/eval_jaxpr/ppermute | solution.py:22
  147.1 2.4 collective-permute-done.2
  150.6 6.3 %collective-permute-done.3 = bf16[2,2,128,512]{2,3,1,0:T(8,128)(2,1)} collective-permute-done((bf16[2,2,128,512]{2,3,1,0:T(8,128)(2,1)}, bf16[2,2,128,512]{2,3,1,0:T(8,128)(2,1)}, u32[]{:S(2)}, u32[]{:S(2)}) %collective-permute-start.3) | collective-permute-done | bytes 524320 | tf_op jit(solution)/shard_map/while/body/eval_jaxpr/ppermute | solution.py:22
  162.3 14.8 %collective-permute-start = (bf16[2,2,128,512]{3,2,1,0:T(8,128)(2,1)}, bf16[2,2,128,512]{3,2,1,0:T(8,128)(2,1)}, u32[]{:S(2)}, u32[]{:S(2)}) collective-permute-start(bf16[2,2,128,512]{3,2,1,0:T(8,128)(2,1)} %bitcast.168), channel_id=1, source_target_pairs={{0,4},{4,8},{8,12},{12,16},{16,20},{20,24},{24,28},{1,5},{5,9},{9,... | collective-permute-start | bytes 1572872 | tf_op jit(solution)/shard_map/while/body/eval_jaxpr/ppermute | solution.py:37
  177.4 6.1 %collective-permute-done = bf16[2,2,128,512]{3,2,1,0:T(8,128)(2,1)} collective-permute-done((bf16[2,2,128,512]{3,2,1,0:T(8,128)(2,1)}, bf16[2,2,128,512]{3,2,1,0:T(8,128)(2,1)}, u32[]{:S(2)}, u32[]{:S(2)}) %collective-permute-start) | collective-permute-done | bytes 524320 | tf_op jit(solution)/shard_map/while/body/eval_jaxpr/ppermute | solution.py:37
  188.8 3.3 collective-permute-start.2
  192.1 7.6 %collective-permute-done.1 = bf16[2,2,128,512]{2,3,1,0:T(8,128)(2,1)} collective-permute-done((bf16[2,2,128,512]{2,3,1,0:T(8,128)(2,1)}, bf16[2,2,128,512]{2,3,1,0:T(8,128)(2,1)}, u32[]{:S(2)}, u32[]{:S(2)}) %collective-permute-start.1) | collective-permute-done | bytes 524320 | tf_op jit(solution)/shard_map/while/body/eval_jaxpr/ppermute | solution.py:22
  200.9 4.3 collective-permute-done.2
  206.4 4.4 collective-permute-done.3
  216.2 16.6 %collective-permute-start = (bf16[2,2,128,512]{3,2,1,0:T(8,128)(2,1)}, bf16[2,2,128,512]{3,2,1,0:T(8,128)(2,1)}, u32[]{:S(2)}, u32[]{:S(2)}) collective-permute-start(bf16[2,2,128,512]{3,2,1,0:T(8,128)(2,1)} %bitcast.168), channel_id=1, source_target_pairs={{0,4},{4,8},{8,12},{12,16},{16,20},{20,24},{24,28},{1,5},{5,9},{9,... | collective-permute-start | bytes 1572872 | tf_op jit(solution)/shard_map/while/body/eval_jaxpr/ppermute | solution.py:37
  233.2 6.1 %collective-permute-done = bf16[2,2,128,512]{3,2,1,0:T(8,128)(2,1)} collective-permute-done((bf16[2,2,128,512]{3,2,1,0:T(8,128)(2,1)}, bf16[2,2,128,512]{3,2,1,0:T(8,128)(2,1)}, u32[]{:S(2)}, u32[]{:S(2)}) %collective-permute-start) | collective-permute-done | bytes 524320 | tf_op jit(solution)/shard_map/while/body/eval_jaxpr/ppermute | solution.py:37
  244.6 3.3 collective-permute-start.2
  247.9 7.0 %collective-permute-done.1 = bf16[2,2,128,512]{2,3,1,0:T(8,128)(2,1)} collective-permute-done((bf16[2,2,128,512]{2,3,1,0:T(8,128)(2,1)}, bf16[2,2,128,512]{2,3,1,0:T(8,128)(2,1)}, u32[]{:S(2)}, u32[]{:S(2)}) %collective-permute-start.1) | collective-permute-done | bytes 524320 | tf_op jit(solution)/shard_map/while/body/eval_jaxpr/ppermute | solution.py:22
  256.0 3.1 collective-permute-done.2
  260.3 5.7 %collective-permute-done.3 = bf16[2,2,128,512]{2,3,1,0:T(8,128)(2,1)} collective-permute-done((bf16[2,2,128,512]{2,3,1,0:T(8,128)(2,1)}, bf16[2,2,128,512]{2,3,1,0:T(8,128)(2,1)}, u32[]{:S(2)}, u32[]{:S(2)}) %collective-permute-start.3) | collective-permute-done | bytes 524320 | tf_op jit(solution)/shard_map/while/body/eval_jaxpr/ppermute | solution.py:22
  271.3 14.8 %collective-permute-start = (bf16[2,2,128,512]{3,2,1,0:T(8,128)(2,1)}, bf16[2,2,128,512]{3,2,1,0:T(8,128)(2,1)}, u32[]{:S(2)}, u32[]{:S(2)}) collective-permute-start(bf16[2,2,128,512]{3,2,1,0:T(8,128)(2,1)} %bitcast.168), channel_id=1, source_target_pairs={{0,4},{4,8},{8,12},{12,16},{16,20},{20,24},{24,28},{1,5},{5,9},{9,... | collective-permute-start | bytes 1572872 | tf_op jit(solution)/shard_map/while/body/eval_jaxpr/ppermute | solution.py:37
  286.4 6.1 %collective-permute-done = bf16[2,2,128,512]{3,2,1,0:T(8,128)(2,1)} collective-permute-done((bf16[2,2,128,512]{3,2,1,0:T(8,128)(2,1)}, bf16[2,2,128,512]{3,2,1,0:T(8,128)(2,1)}, u32[]{:S(2)}, u32[]{:S(2)}) %collective-permute-start) | collective-permute-done | bytes 524320 | tf_op jit(solution)/shard_map/while/body/eval_jaxpr/ppermute | solution.py:37
  297.9 3.3 collective-permute-start.2
  301.1 7.6 %collective-permute-done.1 = bf16[2,2,128,512]{2,3,1,0:T(8,128)(2,1)} collective-permute-done((bf16[2,2,128,512]{2,3,1,0:T(8,128)(2,1)}, bf16[2,2,128,512]{2,3,1,0:T(8,128)(2,1)}, u32[]{:S(2)}, u32[]{:S(2)}) %collective-permute-start.1) | collective-permute-done | bytes 524320 | tf_op jit(solution)/shard_map/while/body/eval_jaxpr/ppermute | solution.py:22
  309.9 4.3 collective-permute-done.2
  315.4 4.4 collective-permute-done.3
  325.1 14.2 %collective-permute-start = (bf16[2,2,128,512]{3,2,1,0:T(8,128)(2,1)}, bf16[2,2,128,512]{3,2,1,0:T(8,128)(2,1)}, u32[]{:S(2)}, u32[]{:S(2)}) collective-permute-start(bf16[2,2,128,512]{3,2,1,0:T(8,128)(2,1)} %bitcast.168), channel_id=1, source_target_pairs={{0,4},{4,8},{8,12},{12,16},{16,20},{20,24},{24,28},{1,5},{5,9},{9,... | collective-permute-start | bytes 1572872 | tf_op jit(solution)/shard_map/while/body/eval_jaxpr/ppermute | solution.py:37
  339.7 6.1 %collective-permute-done = bf16[2,2,128,512]{3,2,1,0:T(8,128)(2,1)} collective-permute-done((bf16[2,2,128,512]{3,2,1,0:T(8,128)(2,1)}, bf16[2,2,128,512]{3,2,1,0:T(8,128)(2,1)}, u32[]{:S(2)}, u32[]{:S(2)}) %collective-permute-start) | collective-permute-done | bytes 524320 | tf_op jit(solution)/shard_map/while/body/eval_jaxpr/ppermute | solution.py:37
  351.2 3.3 collective-permute-start.2
  354.4 8.1 %collective-permute-done.1 = bf16[2,2,128,512]{2,3,1,0:T(8,128)(2,1)} collective-permute-done((bf16[2,2,128,512]{2,3,1,0:T(8,128)(2,1)}, bf16[2,2,128,512]{2,3,1,0:T(8,128)(2,1)}, u32[]{:S(2)}, u32[]{:S(2)}) %collective-permute-start.1) | collective-permute-done | bytes 524320 | tf_op jit(solution)/shard_map/while/body/eval_jaxpr/ppermute | solution.py:22
  363.7 4.3 collective-permute-done.2
  369.2 4.5 collective-permute-done.3
  378.9 13.7 %collective-permute-start = (bf16[2,2,128,512]{3,2,1,0:T(8,128)(2,1)}, bf16[2,2,128,512]{3,2,1,0:T(8,128)(2,1)}, u32[]{:S(2)}, u32[]{:S(2)}) collective-permute-start(bf16[2,2,128,512]{3,2,1,0:T(8,128)(2,1)} %bitcast.168), channel_id=1, source_target_pairs={{0,4},{4,8},{8,12},{12,16},{16,20},{20,24},{24,28},{1,5},{5,9},{9,... | collective-permute-start | bytes 1572872 | tf_op jit(solution)/shard_map/while/body/eval_jaxpr/ppermute | solution.py:37
  393.1 6.1 %collective-permute-done = bf16[2,2,128,512]{3,2,1,0:T(8,128)(2,1)} collective-permute-done((bf16[2,2,128,512]{3,2,1,0:T(8,128)(2,1)}, bf16[2,2,128,512]{3,2,1,0:T(8,128)(2,1)}, u32[]{:S(2)}, u32[]{:S(2)}) %collective-permute-start) | collective-permute-done | bytes 524320 | tf_op jit(solution)/shard_map/while/body/eval_jaxpr/ppermute | solution.py:37
  404.5 3.3 collective-permute-start.2
  407.8 8.6 %collective-permute-done.1 = bf16[2,2,128,512]{2,3,1,0:T(8,128)(2,1)} collective-permute-done((bf16[2,2,128,512]{2,3,1,0:T(8,128)(2,1)}, bf16[2,2,128,512]{2,3,1,0:T(8,128)(2,1)}, u32[]{:S(2)}, u32[]{:S(2)}) %collective-permute-start.1) | collective-permute-done | bytes 524320 | tf_op jit(solution)/shard_map/while/body/eval_jaxpr/ppermute | solution.py:22
  417.5 4.3 collective-permute-done.2
  423.0 4.5 collective-permute-done.3
  432.1 2.1 collective-permute-start.8
  434.1 13.2 %collective-permute-start.7 = (bf16[2,1,2,128,512]{4,3,2,1,0:T(8,128)(2,1)S(1)}, bf16[2,1,2,128,512]{4,3,2,1,0:T(8,128)(2,1)S(1)}, u32[]{:S(2)}, u32[]{:S(2)}) collective-permute-start(bf16[2,1,2,128,512]{4,3,2,1,0:T(8,128)(2,1)S(1)} %convert_element_type.52), channel_id=1, source_target_pairs={{0,4},{4,8},{8,12},{12,16},{16,20},{20,24},{24,28},{1,5},{5,9},{9,... | collective-permute-start | bytes 1572872 | tf_op jit(solution)/shard_map/ppermute | solution.py:48
  448.0 8.1 %collective-permute-done.8 = bf16[2,1,2,128,512]{4,3,2,1,0:T(8,128)(2,1)S(1)} collective-permute-done((bf16[2,1,2,128,512]{4,3,2,1,0:T(8,128)(2,1)S(1)}, bf16[2,1,2,128,512]{4,3,2,1,0:T(8,128)(2,1)S(1)}, u32[]{:S(2)}, u32[]{:S(2)}) %collective-permute-start.8) | collective-permute-done | bytes 524320 | tf_op jit(solution)/shard_map/ppermute | solution.py:50
  456.2 1.3 collective-permute-start.10
  457.5 4.2 collective-permute-start.9
  463.0 5.4 %fusion.68 = f32[2,1,2,128,512]{4,3,2,1,0:T(8,128)S(1)} fusion(f32[2,3,2,130,512]{4,3,2,1,0:T(8,128)S(1)} %maximum_convert_fusion), kind=kLoop, calls=%fused_computation.105 | loop fusion | flops 13369344 | bytes 12779520 | tf_op jit(solution)/shard_map/add | solution.py:118
  (243 shorter events, 100.1 us)
Async XLA Ops:
  0.6 1.5 copy-start
  3.6 19.0 %copy-start.6 = (f32[2,1,2,128,512]{4,3,2,1,0:T(8,128)S(1)}, f32[2,1,2,128,512]{4,3,2,1,0:T(8,128)}, u32[]{:S(2)}) copy-start(f32[2,1,2,128,512]{4,3,2,1,0:T(8,128)} %param.7) | copy-start | bytes 3145732
  6.4 16.1 %collective-permute-start.4 = (bf16[2,2,128,512]{2,3,1,0:T(8,128)(2,1)}, bf16[2,2,128,512]{2,3,1,0:T(8,128)(2,1)}, u32[]{:S(2)}, u32[]{:S(2)}) collective-permute-start(bf16[2,2,128,512]{2,3,1,0:T(8,128)(2,1)} %get-tuple-element.103), channel_id=1, source_target_pairs={{0,1},{1,2},{2,3},{3,0},{4,5},{5,6},{6,7},{7,4},{8,9},{9,10},{10,1... | collective-permute-start | bytes 1572872 | tf_op jit(solution)/shard_map/ppermute | solution.py:22
  8.5 24.8 %collective-permute-start.5 = (bf16[2,2,128,512]{2,3,1,0:T(8,128)(2,1)}, bf16[2,2,128,512]{2,3,1,0:T(8,128)(2,1)}, u32[]{:S(2)}, u32[]{:S(2)}) collective-permute-start(bf16[2,2,128,512]{2,3,1,0:T(8,128)(2,1)} %get-tuple-element.103), channel_id=1, source_target_pairs={{0,3},{1,0},{2,1},{3,2},{4,7},{5,4},{6,5},{7,6},{8,11},{9,8},{10,9... | collective-permute-start | bytes 1572872 | tf_op jit(solution)/shard_map/ppermute | solution.py:27
  22.5 20.4 %collective-permute-start.6 = (bf16[2,2,128,512]{2,3,1,0:T(8,128)(2,1)}, bf16[2,2,128,512]{2,3,1,0:T(8,128)(2,1)}, u32[]{:S(2)}, u32[]{:S(2)}) collective-permute-start(bf16[2,2,128,512]{2,3,1,0:T(8,128)(2,1)} %collective-permute-done.4), channel_id=1, source_target_pairs={{0,1},{1,2},{2,3},{3,0},{4,5},{5,6},{6,7},{7,4},{8,9},{9,10},{10,1... | collective-permute-start | bytes 1572872 | tf_op jit(solution)/shard_map/ppermute | solution.py:22
  22.9 22.0 %copy-start.4 = (bf16[1,2,128,512]{3,2,1,0:T(8,128)(2,1)S(1)}, bf16[1,2,128,512]{3,2,1,0:T(8,128)(2,1)}, u32[]{:S(2)}) copy-start(bf16[1,2,128,512]{3,2,1,0:T(8,128)(2,1)} %param.11) | copy-start | bytes 786436
  51.6 7.8 %copy-start.1 = (f32[2,1,2,128,512]{3,4,2,0,1:T(8,128)}, f32[2,1,2,128,512]{3,4,2,0,1:T(8,128)S(1)}, u32[]{:S(2)}) copy-start(f32[2,1,2,128,512]{3,4,2,0,1:T(8,128)S(1)} %get-tuple-element.178) | copy-start | bytes 3145732 | tf_op jit(solution)/shard_map/while
  52.7 12.7 %collective-permute-start = (bf16[2,2,128,512]{3,2,1,0:T(8,128)(2,1)}, bf16[2,2,128,512]{3,2,1,0:T(8,128)(2,1)}, u32[]{:S(2)}, u32[]{:S(2)}) collective-permute-start(bf16[2,2,128,512]{3,2,1,0:T(8,128)(2,1)} %bitcast.168), channel_id=1, source_target_pairs={{0,4},{4,8},{8,12},{12,16},{16,20},{20,24},{24,28},{1,5},{5,9},{9,... | collective-permute-start | bytes 1572872 | tf_op jit(solution)/shard_map/while/body/eval_jaxpr/ppermute | solution.py:37
  68.9 0.9 copy-start.3
  70.8 33.6 %copy-start.5 = (bf16[1,2,128,512]{3,2,1,0:T(8,128)(2,1)S(1)}, bf16[1,2,128,512]{3,2,1,0:T(8,128)(2,1)}, u32[]{:S(2)}) copy-start(bf16[1,2,128,512]{3,2,1,0:T(8,128)(2,1)} %get-tuple-element.180) | copy-start | bytes 786436 | tf_op jit(solution)/shard_map/while
  70.8 16.1 %collective-permute-start.1 = (bf16[2,2,128,512]{2,3,1,0:T(8,128)(2,1)}, bf16[2,2,128,512]{2,3,1,0:T(8,128)(2,1)}, u32[]{:S(2)}, u32[]{:S(2)}) collective-permute-start(bf16[2,2,128,512]{2,3,1,0:T(8,128)(2,1)} %get-tuple-element.145), channel_id=1, source_target_pairs={{0,1},{1,2},{2,3},{3,0},{4,5},{5,6},{6,7},{7,4},{8,9},{9,10},{10,1... | collective-permute-start | bytes 1572872 | tf_op jit(solution)/shard_map/while/body/eval_jaxpr/ppermute | solution.py:22
  70.8 23.6 %collective-permute-start.2 = (bf16[2,2,128,512]{2,3,1,0:T(8,128)(2,1)}, bf16[2,2,128,512]{2,3,1,0:T(8,128)(2,1)}, u32[]{:S(2)}, u32[]{:S(2)}) collective-permute-start(bf16[2,2,128,512]{2,3,1,0:T(8,128)(2,1)} %get-tuple-element.145), channel_id=1, source_target_pairs={{0,3},{1,0},{2,1},{3,2},{4,7},{5,4},{6,5},{7,6},{8,11},{9,8},{10,9... | collective-permute-start | bytes 1572872 | tf_op jit(solution)/shard_map/while/body/eval_jaxpr/ppermute | solution.py:27
  86.8 16.4 %collective-permute-start.3 = (bf16[2,2,128,512]{2,3,1,0:T(8,128)(2,1)}, bf16[2,2,128,512]{2,3,1,0:T(8,128)(2,1)}, u32[]{:S(2)}, u32[]{:S(2)}) collective-permute-start(bf16[2,2,128,512]{2,3,1,0:T(8,128)(2,1)} %collective-permute-done.1), channel_id=1, source_target_pairs={{0,1},{1,2},{2,3},{3,0},{4,5},{5,6},{6,7},{7,4},{8,9},{9,10},{10,1... | collective-permute-start | bytes 1572872 | tf_op jit(solution)/shard_map/while/body/eval_jaxpr/ppermute | solution.py:22
  106.2 1.2 copy-start.2
  107.4 11.0 %copy-start.1 = (f32[2,1,2,128,512]{3,4,2,0,1:T(8,128)}, f32[2,1,2,128,512]{3,4,2,0,1:T(8,128)S(1)}, u32[]{:S(2)}) copy-start(f32[2,1,2,128,512]{3,4,2,0,1:T(8,128)S(1)} %get-tuple-element.178) | copy-start | bytes 3145732 | tf_op jit(solution)/shard_map/while
  108.5 15.9 %collective-permute-start = (bf16[2,2,128,512]{3,2,1,0:T(8,128)(2,1)}, bf16[2,2,128,512]{3,2,1,0:T(8,128)(2,1)}, u32[]{:S(2)}, u32[]{:S(2)}) collective-permute-start(bf16[2,2,128,512]{3,2,1,0:T(8,128)(2,1)} %bitcast.168), channel_id=1, source_target_pairs={{0,4},{4,8},{8,12},{12,16},{16,20},{20,24},{24,28},{1,5},{5,9},{9,... | collective-permute-start | bytes 1572872 | tf_op jit(solution)/shard_map/while/body/eval_jaxpr/ppermute | solution.py:37
  128.0 0.9 copy-start.3
  129.8 28.3 %copy-start.5 = (bf16[1,2,128,512]{3,2,1,0:T(8,128)(2,1)S(1)}, bf16[1,2,128,512]{3,2,1,0:T(8,128)(2,1)}, u32[]{:S(2)}) copy-start(bf16[1,2,128,512]{3,2,1,0:T(8,128)(2,1)} %get-tuple-element.180) | copy-start | bytes 786436 | tf_op jit(solution)/shard_map/while
  129.8 16.1 %collective-permute-start.1 = (bf16[2,2,128,512]{2,3,1,0:T(8,128)(2,1)}, bf16[2,2,128,512]{2,3,1,0:T(8,128)(2,1)}, u32[]{:S(2)}, u32[]{:S(2)}) collective-permute-start(bf16[2,2,128,512]{2,3,1,0:T(8,128)(2,1)} %get-tuple-element.145), channel_id=1, source_target_pairs={{0,1},{1,2},{2,3},{3,0},{4,5},{5,6},{6,7},{7,4},{8,9},{9,10},{10,1... | collective-permute-start | bytes 1572872 | tf_op jit(solution)/shard_map/while/body/eval_jaxpr/ppermute | solution.py:22
  129.8 19.6 %collective-permute-start.2 = (bf16[2,2,128,512]{2,3,1,0:T(8,128)(2,1)}, bf16[2,2,128,512]{2,3,1,0:T(8,128)(2,1)}, u32[]{:S(2)}, u32[]{:S(2)}) collective-permute-start(bf16[2,2,128,512]{2,3,1,0:T(8,128)(2,1)} %get-tuple-element.145), channel_id=1, source_target_pairs={{0,3},{1,0},{2,1},{3,2},{4,7},{5,4},{6,5},{7,6},{8,11},{9,8},{10,9... | collective-permute-start | bytes 1572872 | tf_op jit(solution)/shard_map/while/body/eval_jaxpr/ppermute | solution.py:27
  145.9 11.1 %collective-permute-start.3 = (bf16[2,2,128,512]{2,3,1,0:T(8,128)(2,1)}, bf16[2,2,128,512]{2,3,1,0:T(8,128)(2,1)}, u32[]{:S(2)}, u32[]{:S(2)}) collective-permute-start(bf16[2,2,128,512]{2,3,1,0:T(8,128)(2,1)} %collective-permute-done.1), channel_id=1, source_target_pairs={{0,1},{1,2},{2,3},{3,0},{4,5},{5,6},{6,7},{7,4},{8,9},{9,10},{10,1... | collective-permute-start | bytes 1572872 | tf_op jit(solution)/shard_map/while/body/eval_jaxpr/ppermute | solution.py:22
  159.9 1.2 copy-start.2
  161.1 16.3 %copy-start.1 = (f32[2,1,2,128,512]{3,4,2,0,1:T(8,128)}, f32[2,1,2,128,512]{3,4,2,0,1:T(8,128)S(1)}, u32[]{:S(2)}) copy-start(f32[2,1,2,128,512]{3,4,2,0,1:T(8,128)S(1)} %get-tuple-element.178) | copy-start | bytes 3145732 | tf_op jit(solution)/shard_map/while
  162.3 21.2 %collective-permute-start = (bf16[2,2,128,512]{3,2,1,0:T(8,128)(2,1)}, bf16[2,2,128,512]{3,2,1,0:T(8,128)(2,1)}, u32[]{:S(2)}, u32[]{:S(2)}) collective-permute-start(bf16[2,2,128,512]{3,2,1,0:T(8,128)(2,1)} %bitcast.168), channel_id=1, source_target_pairs={{0,4},{4,8},{8,12},{12,16},{16,20},{20,24},{24,28},{1,5},{5,9},{9,... | collective-permute-start | bytes 1572872 | tf_op jit(solution)/shard_map/while/body/eval_jaxpr/ppermute | solution.py:37
  188.8 23.2 %copy-start.5 = (bf16[1,2,128,512]{3,2,1,0:T(8,128)(2,1)S(1)}, bf16[1,2,128,512]{3,2,1,0:T(8,128)(2,1)}, u32[]{:S(2)}) copy-start(bf16[1,2,128,512]{3,2,1,0:T(8,128)(2,1)} %get-tuple-element.180) | copy-start | bytes 786436 | tf_op jit(solution)/shard_map/while
  188.8 10.9 %collective-permute-start.1 = (bf16[2,2,128,512]{2,3,1,0:T(8,128)(2,1)}, bf16[2,2,128,512]{2,3,1,0:T(8,128)(2,1)}, u32[]{:S(2)}, u32[]{:S(2)}) collective-permute-start(bf16[2,2,128,512]{2,3,1,0:T(8,128)(2,1)} %get-tuple-element.145), channel_id=1, source_target_pairs={{0,1},{1,2},{2,3},{3,0},{4,5},{5,6},{6,7},{7,4},{8,9},{9,10},{10,1... | collective-permute-start | bytes 1572872 | tf_op jit(solution)/shard_map/while/body/eval_jaxpr/ppermute | solution.py:22
  188.8 16.4 %collective-permute-start.2 = (bf16[2,2,128,512]{2,3,1,0:T(8,128)(2,1)}, bf16[2,2,128,512]{2,3,1,0:T(8,128)(2,1)}, u32[]{:S(2)}, u32[]{:S(2)}) collective-permute-start(bf16[2,2,128,512]{2,3,1,0:T(8,128)(2,1)} %get-tuple-element.145), channel_id=1, source_target_pairs={{0,3},{1,0},{2,1},{3,2},{4,7},{5,4},{6,5},{7,6},{8,11},{9,8},{10,9... | collective-permute-start | bytes 1572872 | tf_op jit(solution)/shard_map/while/body/eval_jaxpr/ppermute | solution.py:27
  199.7 11.1 %collective-permute-start.3 = (bf16[2,2,128,512]{2,3,1,0:T(8,128)(2,1)}, bf16[2,2,128,512]{2,3,1,0:T(8,128)(2,1)}, u32[]{:S(2)}, u32[]{:S(2)}) collective-permute-start(bf16[2,2,128,512]{2,3,1,0:T(8,128)(2,1)} %collective-permute-done.1), channel_id=1, source_target_pairs={{0,1},{1,2},{2,3},{3,0},{4,5},{5,6},{6,7},{7,4},{8,9},{9,10},{10,1... | collective-permute-start | bytes 1572872 | tf_op jit(solution)/shard_map/while/body/eval_jaxpr/ppermute | solution.py:22
  213.8 1.2 copy-start.2
  215.0 18.1 %copy-start.1 = (f32[2,1,2,128,512]{3,4,2,0,1:T(8,128)}, f32[2,1,2,128,512]{3,4,2,0,1:T(8,128)S(1)}, u32[]{:S(2)}) copy-start(f32[2,1,2,128,512]{3,4,2,0,1:T(8,128)S(1)} %get-tuple-element.178) | copy-start | bytes 3145732 | tf_op jit(solution)/shard_map/while
  216.2 23.1 %collective-permute-start = (bf16[2,2,128,512]{3,2,1,0:T(8,128)(2,1)}, bf16[2,2,128,512]{3,2,1,0:T(8,128)(2,1)}, u32[]{:S(2)}, u32[]{:S(2)}) collective-permute-start(bf16[2,2,128,512]{3,2,1,0:T(8,128)(2,1)} %bitcast.168), channel_id=1, source_target_pairs={{0,4},{4,8},{8,12},{12,16},{16,20},{20,24},{24,28},{1,5},{5,9},{9,... | collective-permute-start | bytes 1572872 | tf_op jit(solution)/shard_map/while/body/eval_jaxpr/ppermute | solution.py:37
  244.6 22.6 %copy-start.5 = (bf16[1,2,128,512]{3,2,1,0:T(8,128)(2,1)S(1)}, bf16[1,2,128,512]{3,2,1,0:T(8,128)(2,1)}, u32[]{:S(2)}) copy-start(bf16[1,2,128,512]{3,2,1,0:T(8,128)(2,1)} %get-tuple-element.180) | copy-start | bytes 786436 | tf_op jit(solution)/shard_map/while
  244.6 10.2 %collective-permute-start.1 = (bf16[2,2,128,512]{2,3,1,0:T(8,128)(2,1)}, bf16[2,2,128,512]{2,3,1,0:T(8,128)(2,1)}, u32[]{:S(2)}, u32[]{:S(2)}) collective-permute-start(bf16[2,2,128,512]{2,3,1,0:T(8,128)(2,1)} %get-tuple-element.145), channel_id=1, source_target_pairs={{0,1},{1,2},{2,3},{3,0},{4,5},{5,6},{6,7},{7,4},{8,9},{9,10},{10,1... | collective-permute-start | bytes 1572872 | tf_op jit(solution)/shard_map/while/body/eval_jaxpr/ppermute | solution.py:22
  244.6 14.6 %collective-permute-start.2 = (bf16[2,2,128,512]{2,3,1,0:T(8,128)(2,1)}, bf16[2,2,128,512]{2,3,1,0:T(8,128)(2,1)}, u32[]{:S(2)}, u32[]{:S(2)}) collective-permute-start(bf16[2,2,128,512]{2,3,1,0:T(8,128)(2,1)} %get-tuple-element.145), channel_id=1, source_target_pairs={{0,3},{1,0},{2,1},{3,2},{4,7},{5,4},{6,5},{7,6},{8,11},{9,8},{10,9... | collective-permute-start | bytes 1572872 | tf_op jit(solution)/shard_map/while/body/eval_jaxpr/ppermute | solution.py:27
  254.8 11.2 %collective-permute-start.3 = (bf16[2,2,128,512]{2,3,1,0:T(8,128)(2,1)}, bf16[2,2,128,512]{2,3,1,0:T(8,128)(2,1)}, u32[]{:S(2)}, u32[]{:S(2)}) collective-permute-start(bf16[2,2,128,512]{2,3,1,0:T(8,128)(2,1)} %collective-permute-done.1), channel_id=1, source_target_pairs={{0,1},{1,2},{2,3},{3,0},{4,5},{5,6},{6,7},{7,4},{8,9},{9,10},{10,1... | collective-permute-start | bytes 1572872 | tf_op jit(solution)/shard_map/while/body/eval_jaxpr/ppermute | solution.py:22
  268.9 1.2 copy-start.2
  270.1 16.3 %copy-start.1 = (f32[2,1,2,128,512]{3,4,2,0,1:T(8,128)}, f32[2,1,2,128,512]{3,4,2,0,1:T(8,128)S(1)}, u32[]{:S(2)}) copy-start(f32[2,1,2,128,512]{3,4,2,0,1:T(8,128)S(1)} %get-tuple-element.178) | copy-start | bytes 3145732 | tf_op jit(solution)/shard_map/while
  271.3 21.2 %collective-permute-start = (bf16[2,2,128,512]{3,2,1,0:T(8,128)(2,1)}, bf16[2,2,128,512]{3,2,1,0:T(8,128)(2,1)}, u32[]{:S(2)}, u32[]{:S(2)}) collective-permute-start(bf16[2,2,128,512]{3,2,1,0:T(8,128)(2,1)} %bitcast.168), channel_id=1, source_target_pairs={{0,4},{4,8},{8,12},{12,16},{16,20},{20,24},{24,28},{1,5},{5,9},{9,... | collective-permute-start | bytes 1572872 | tf_op jit(solution)/shard_map/while/body/eval_jaxpr/ppermute | solution.py:37
  297.9 23.2 %copy-start.5 = (bf16[1,2,128,512]{3,2,1,0:T(8,128)(2,1)S(1)}, bf16[1,2,128,512]{3,2,1,0:T(8,128)(2,1)}, u32[]{:S(2)}) copy-start(bf16[1,2,128,512]{3,2,1,0:T(8,128)(2,1)} %get-tuple-element.180) | copy-start | bytes 786436 | tf_op jit(solution)/shard_map/while
  297.9 10.9 %collective-permute-start.1 = (bf16[2,2,128,512]{2,3,1,0:T(8,128)(2,1)}, bf16[2,2,128,512]{2,3,1,0:T(8,128)(2,1)}, u32[]{:S(2)}, u32[]{:S(2)}) collective-permute-start(bf16[2,2,128,512]{2,3,1,0:T(8,128)(2,1)} %get-tuple-element.145), channel_id=1, source_target_pairs={{0,1},{1,2},{2,3},{3,0},{4,5},{5,6},{6,7},{7,4},{8,9},{9,10},{10,1... | collective-permute-start | bytes 1572872 | tf_op jit(solution)/shard_map/while/body/eval_jaxpr/ppermute | solution.py:22
  297.9 16.4 %collective-permute-start.2 = (bf16[2,2,128,512]{2,3,1,0:T(8,128)(2,1)}, bf16[2,2,128,512]{2,3,1,0:T(8,128)(2,1)}, u32[]{:S(2)}, u32[]{:S(2)}) collective-permute-start(bf16[2,2,128,512]{2,3,1,0:T(8,128)(2,1)} %get-tuple-element.145), channel_id=1, source_target_pairs={{0,3},{1,0},{2,1},{3,2},{4,7},{5,4},{6,5},{7,6},{8,11},{9,8},{10,9... | collective-permute-start | bytes 1572872 | tf_op jit(solution)/shard_map/while/body/eval_jaxpr/ppermute | solution.py:27
  308.7 11.1 %collective-permute-start.3 = (bf16[2,2,128,512]{2,3,1,0:T(8,128)(2,1)}, bf16[2,2,128,512]{2,3,1,0:T(8,128)(2,1)}, u32[]{:S(2)}, u32[]{:S(2)}) collective-permute-start(bf16[2,2,128,512]{2,3,1,0:T(8,128)(2,1)} %collective-permute-done.1), channel_id=1, source_target_pairs={{0,1},{1,2},{2,3},{3,0},{4,5},{5,6},{6,7},{7,4},{8,9},{9,10},{10,1... | collective-permute-start | bytes 1572872 | tf_op jit(solution)/shard_map/while/body/eval_jaxpr/ppermute | solution.py:22
  322.8 1.2 copy-start.2
  324.0 15.7 %copy-start.1 = (f32[2,1,2,128,512]{3,4,2,0,1:T(8,128)}, f32[2,1,2,128,512]{3,4,2,0,1:T(8,128)S(1)}, u32[]{:S(2)}) copy-start(f32[2,1,2,128,512]{3,4,2,0,1:T(8,128)S(1)} %get-tuple-element.178) | copy-start | bytes 3145732 | tf_op jit(solution)/shard_map/while
  325.1 20.7 %collective-permute-start = (bf16[2,2,128,512]{3,2,1,0:T(8,128)(2,1)}, bf16[2,2,128,512]{3,2,1,0:T(8,128)(2,1)}, u32[]{:S(2)}, u32[]{:S(2)}) collective-permute-start(bf16[2,2,128,512]{3,2,1,0:T(8,128)(2,1)} %bitcast.168), channel_id=1, source_target_pairs={{0,4},{4,8},{8,12},{12,16},{16,20},{20,24},{24,28},{1,5},{5,9},{9,... | collective-permute-start | bytes 1572872 | tf_op jit(solution)/shard_map/while/body/eval_jaxpr/ppermute | solution.py:37
  351.2 23.7 %copy-start.5 = (bf16[1,2,128,512]{3,2,1,0:T(8,128)(2,1)S(1)}, bf16[1,2,128,512]{3,2,1,0:T(8,128)(2,1)}, u32[]{:S(2)}) copy-start(bf16[1,2,128,512]{3,2,1,0:T(8,128)(2,1)} %get-tuple-element.180) | copy-start | bytes 786436 | tf_op jit(solution)/shard_map/while
  351.2 11.3 %collective-permute-start.1 = (bf16[2,2,128,512]{2,3,1,0:T(8,128)(2,1)}, bf16[2,2,128,512]{2,3,1,0:T(8,128)(2,1)}, u32[]{:S(2)}, u32[]{:S(2)}) collective-permute-start(bf16[2,2,128,512]{2,3,1,0:T(8,128)(2,1)} %get-tuple-element.145), channel_id=1, source_target_pairs={{0,1},{1,2},{2,3},{3,0},{4,5},{5,6},{6,7},{7,4},{8,9},{9,10},{10,1... | collective-permute-start | bytes 1572872 | tf_op jit(solution)/shard_map/while/body/eval_jaxpr/ppermute | solution.py:22
  351.2 16.8 %collective-permute-start.2 = (bf16[2,2,128,512]{2,3,1,0:T(8,128)(2,1)}, bf16[2,2,128,512]{2,3,1,0:T(8,128)(2,1)}, u32[]{:S(2)}, u32[]{:S(2)}) collective-permute-start(bf16[2,2,128,512]{2,3,1,0:T(8,128)(2,1)} %get-tuple-element.145), channel_id=1, source_target_pairs={{0,3},{1,0},{2,1},{3,2},{4,7},{5,4},{6,5},{7,6},{8,11},{9,8},{10,9... | collective-permute-start | bytes 1572872 | tf_op jit(solution)/shard_map/while/body/eval_jaxpr/ppermute | solution.py:27
  362.5 11.2 %collective-permute-start.3 = (bf16[2,2,128,512]{2,3,1,0:T(8,128)(2,1)}, bf16[2,2,128,512]{2,3,1,0:T(8,128)(2,1)}, u32[]{:S(2)}, u32[]{:S(2)}) collective-permute-start(bf16[2,2,128,512]{2,3,1,0:T(8,128)(2,1)} %collective-permute-done.1), channel_id=1, source_target_pairs={{0,1},{1,2},{2,3},{3,0},{4,5},{5,6},{6,7},{7,4},{8,9},{9,10},{10,1... | collective-permute-start | bytes 1572872 | tf_op jit(solution)/shard_map/while/body/eval_jaxpr/ppermute | solution.py:22
  376.6 1.2 copy-start.2
  377.8 15.2 %copy-start.1 = (f32[2,1,2,128,512]{3,4,2,0,1:T(8,128)}, f32[2,1,2,128,512]{3,4,2,0,1:T(8,128)S(1)}, u32[]{:S(2)}) copy-start(f32[2,1,2,128,512]{3,4,2,0,1:T(8,128)S(1)} %get-tuple-element.178) | copy-start | bytes 3145732 | tf_op jit(solution)/shard_map/while
  378.9 20.2 %collective-permute-start = (bf16[2,2,128,512]{3,2,1,0:T(8,128)(2,1)}, bf16[2,2,128,512]{3,2,1,0:T(8,128)(2,1)}, u32[]{:S(2)}, u32[]{:S(2)}) collective-permute-start(bf16[2,2,128,512]{3,2,1,0:T(8,128)(2,1)} %bitcast.168), channel_id=1, source_target_pairs={{0,4},{4,8},{8,12},{12,16},{16,20},{20,24},{24,28},{1,5},{5,9},{9,... | collective-permute-start | bytes 1572872 | tf_op jit(solution)/shard_map/while/body/eval_jaxpr/ppermute | solution.py:37
  404.5 24.2 %copy-start.5 = (bf16[1,2,128,512]{3,2,1,0:T(8,128)(2,1)S(1)}, bf16[1,2,128,512]{3,2,1,0:T(8,128)(2,1)}, u32[]{:S(2)}) copy-start(bf16[1,2,128,512]{3,2,1,0:T(8,128)(2,1)} %get-tuple-element.180) | copy-start | bytes 786436 | tf_op jit(solution)/shard_map/while
  404.5 11.8 %collective-permute-start.1 = (bf16[2,2,128,512]{2,3,1,0:T(8,128)(2,1)}, bf16[2,2,128,512]{2,3,1,0:T(8,128)(2,1)}, u32[]{:S(2)}, u32[]{:S(2)}) collective-permute-start(bf16[2,2,128,512]{2,3,1,0:T(8,128)(2,1)} %get-tuple-element.145), channel_id=1, source_target_pairs={{0,1},{1,2},{2,3},{3,0},{4,5},{5,6},{6,7},{7,4},{8,9},{9,10},{10,1... | collective-permute-start | bytes 1572872 | tf_op jit(solution)/shard_map/while/body/eval_jaxpr/ppermute | solution.py:22
  404.5 17.3 %collective-permute-start.2 = (bf16[2,2,128,512]{2,3,1,0:T(8,128)(2,1)}, bf16[2,2,128,512]{2,3,1,0:T(8,128)(2,1)}, u32[]{:S(2)}, u32[]{:S(2)}) collective-permute-start(bf16[2,2,128,512]{2,3,1,0:T(8,128)(2,1)} %get-tuple-element.145), channel_id=1, source_target_pairs={{0,3},{1,0},{2,1},{3,2},{4,7},{5,4},{6,5},{7,6},{8,11},{9,8},{10,9... | collective-permute-start | bytes 1572872 | tf_op jit(solution)/shard_map/while/body/eval_jaxpr/ppermute | solution.py:27
  416.3 11.2 %collective-permute-start.3 = (bf16[2,2,128,512]{2,3,1,0:T(8,128)(2,1)}, bf16[2,2,128,512]{2,3,1,0:T(8,128)(2,1)}, u32[]{:S(2)}, u32[]{:S(2)}) collective-permute-start(bf16[2,2,128,512]{2,3,1,0:T(8,128)(2,1)} %collective-permute-done.1), channel_id=1, source_target_pairs={{0,1},{1,2},{2,3},{3,0},{4,5},{5,6},{6,7},{7,4},{8,9},{9,10},{10,1... | collective-permute-start | bytes 1572872 | tf_op jit(solution)/shard_map/while/body/eval_jaxpr/ppermute | solution.py:22
  430.4 1.2 copy-start.2
  432.0 36.5 %copy-start.8 = (f32[2,1,2,128,512]{4,3,2,1,0:T(8,128)}, f32[2,1,2,128,512]{4,3,2,1,0:T(8,128)S(1)}, u32[]{:S(2)}) copy-start(f32[2,1,2,128,512]{4,3,2,1,0:T(8,128)S(1)} %copy.26) | copy-start | bytes 3145732
  432.0 29.7 %copy-start.9 = (f32[1,128,512]{2,1,0:T(8,128)S(1)}, f32[1,128,512]{2,1,0:T(8,128)}, u32[]{:S(2)}) copy-start(f32[1,128,512]{2,1,0:T(8,128)} %param.8) | copy-start | bytes 786436
  432.1 24.1 %collective-permute-start.8 = (bf16[2,1,2,128,512]{4,3,2,1,0:T(8,128)(2,1)S(1)}, bf16[2,1,2,128,512]{4,3,2,1,0:T(8,128)(2,1)S(1)}, u32[]{:S(2)}, u32[]{:S(2)}) collective-permute-start(bf16[2,1,2,128,512]{4,3,2,1,0:T(8,128)(2,1)S(1)} %convert_element_type.52), channel_id=1, source_target_pairs={{4,0},{8,4},{12,8},{16,12},{20,16},{24,20},{28,24},{5,1},{9,5},{13... | collective-permute-start | bytes 1572872 | tf_op jit(solution)/shard_map/ppermute | solution.py:50
  434.1 22.0 %collective-permute-start.7 = (bf16[2,1,2,128,512]{4,3,2,1,0:T(8,128)(2,1)S(1)}, bf16[2,1,2,128,512]{4,3,2,1,0:T(8,128)(2,1)S(1)}, u32[]{:S(2)}, u32[]{:S(2)}) collective-permute-start(bf16[2,1,2,128,512]{4,3,2,1,0:T(8,128)(2,1)S(1)} %convert_element_type.52), channel_id=1, source_target_pairs={{0,4},{4,8},{8,12},{12,16},{16,20},{20,24},{24,28},{1,5},{5,9},{9,... | collective-permute-start | bytes 1572872 | tf_op jit(solution)/shard_map/ppermute | solution.py:48
  456.2 5.5 %collective-permute-start.10 = (bf16[2,3,2,1,512]{4,3,2,1,0:T(2,128)(2,1)S(1)}, bf16[2,3,2,1,512]{4,3,2,1,0:T(2,128)(2,1)S(1)}, u32[]{:S(2)}, u32[]{:S(2)}) collective-permute-start(bf16[2,3,2,1,512]{4,3,2,1,0:T(2,128)(2,1)S(1)} %get-tuple-element.102), channel_id=1, source_target_pairs={{1,0},{2,1},{3,2},{5,4},{6,5},{7,6},{9,8},{10,9},{11,10},{13,12},{... | collective-permute-start | bytes 36872 | tf_op jit(solution)/shard_map/ppermute | solution.py:50
  457.5 4.9 %collective-permute-start.9 = (bf16[2,3,2,1,512]{4,3,2,1,0:T(2,128)(2,1)S(1)}, bf16[2,3,2,1,512]{4,3,2,1,0:T(2,128)(2,1)S(1)}, u32[]{:S(2)}, u32[]{:S(2)}) collective-permute-start(bf16[2,3,2,1,512]{4,3,2,1,0:T(2,128)(2,1)S(1)} %get-tuple-element.101), channel_id=1, source_target_pairs={{0,1},{1,2},{2,3},{4,5},{5,6},{6,7},{8,9},{9,10},{10,11},{12,13},{... | collective-permute-start | bytes 36872 | tf_op jit(solution)/shard_map/ppermute | solution.py:48
  468.4 1.2 copy-start.7
  (5 other events, 4.8 us)
